TPU v7x, 32 devices: a whole 2x2x4 slice. The times are simulated.
32 devices in a mesh: wide: 16 (over z, x, core), narrow: 2 (over y).
Axes of the slice: x: 2, y: 2, z: 4, core: 2. Of those that a mesh axis runs over, the one named last changes fastest.
Arguments:
- latents: bfloat16 [65536, 1024], P(('wide', 'narrow')), may hold values from -6 to 6
- cotangent: bfloat16 [65536, 1024], P(('wide', 'narrow')), may hold values from -6 to 6
- crop_counts: int32 [16], replicated, may hold values from 1 to 8, as said below
- image_device: int32 [16], replicated, may hold values from 0 to 15, as said below
- query_weight: bfloat16 [1024, 1024], P(None, 'narrow'), may hold values from -0.1875 to 0.1875
- key_weight: bfloat16 [1024, 1024], P(None, 'narrow'), may hold values from -0.1875 to 0.1875
- value_weight: bfloat16 [1024, 1024], P(None, 'narrow'), may hold values from -0.1875 to 0.1875
- out_weight: bfloat16 [1024, 1024], P('narrow'), may hold values from -2 to 2
- up_weight: bfloat16 [1024, 1024], P(None, 'narrow'), may hold values from -0.1875 to 0.1875
- down_weight: bfloat16 [1024, 1024], P('narrow'), may hold values from -0.1875 to 0.1875
- query_bias: bfloat16 [1024], P('narrow'), may hold values from -3 to 3
- value_bias: bfloat16 [1024], P('narrow'), may hold values from -3 to 3
- up_bias: bfloat16 [1024], P('narrow'), may hold values from -3 to 3
- out_bias: float32 [1024], replicated, may hold values from -2 to 2
- down_bias: float32 [1024], replicated, may hold values from -2 to 2
- first_gain: float32 [1024], replicated, may hold values from 0.5 to 1.5
- first_shift: float32 [1024], replicated, may hold values from -1.2 to 1.2
- second_gain: float32 [1024], replicated, may hold values from 0.5 to 1.5
- second_shift: float32 [1024], replicated, may hold values from -1.2 to 1.2
Outputs:
- block_output: bfloat16 [65536, 1024], P(('wide', 'narrow'))
- latents_gradient: float32 [65536, 1024], P(('wide', 'narrow'))
- query_weight_gradient: float32 [1024, 1024], P(None, 'narrow')
- key_weight_gradient: float32 [1024, 1024], P(None, 'narrow')
- value_weight_gradient: float32 [1024, 1024], P(None, 'narrow')
- out_weight_gradient: float32 [1024, 1024], P('narrow')
- up_weight_gradient: float32 [1024, 1024], P(None, 'narrow')
- down_weight_gradient: float32 [1024, 1024], P('narrow')
- query_bias_gradient: float32 [1024], P('narrow')
- value_bias_gradient: float32 [1024], P('narrow')
- up_bias_gradient: float32 [1024], P('narrow')
- out_bias_gradient: float32 [1024], replicated
- down_bias_gradient: float32 [1024], replicated
- first_gain_gradient: float32 [1024], replicated
- first_shift_gradient: float32 [1024], replicated
- second_gain_gradient: float32 [1024], replicated
- second_shift_gradient: float32 [1024], replicated
Inputs may be any that keep to these rules, and one draw needn't show every extreme that they name: `crop_counts`: each image holds 1 to 8 crops; the images of one wide index hold 8 crops or fewer together, and some wide index holds exactly 8. `image_device`: every wide index receives exactly one image.
All inputs are finite; a program needn't handle non-finite values.
Results may differ from a plain program's by a relative error of at most 0.02.
Values may be sent and summed in bfloat16 or wider, within the bound.
No kernel may reach another device: no remote copies, remote signals or barrier semaphores. Data moves between devices by JAX's collectives and lax.ppermute only.
A program may use at most 192 MiB of HBM per device.

v0:
```python
from functools import partial
import math
import jax
import jax.numpy as jnp
from jax import lax
from jax.sharding import PartitionSpec as P

HS = 128
CROP = 512
EPSILON = 1e-05


def normalize(values, gain, shift):
    center = values - jnp.mean(values, axis=-1, keepdims=True)
    inverse = lax.rsqrt(jnp.mean(center * center, axis=-1, keepdims=True) + EPSILON)
    unit = center * inverse
    return (unit * gain + shift, unit, inverse)


def normalize_back(upstream, unit, inverse, gain):
    scaled = upstream * gain
    inner = scaled - jnp.mean(scaled, axis=-1, keepdims=True)
    inner = inner - unit * jnp.mean(scaled * unit, axis=-1, keepdims=True)
    return (inner * inverse, jnp.sum(upstream * unit, axis=0), jnp.sum(upstream, axis=0))


def matmul(left, right):
    return jnp.dot(left, right, preferred_element_type=jnp.float32)


def matmul_left(left, right):
    return lax.dot_general(
        left, right, (((0,), (0,)), ((), ())), preferred_element_type=jnp.float32
    )


def matmul_right(left, right):
    return lax.dot_general(
        left, right, (((1,), (1,)), ((), ())), preferred_element_type=jnp.float32
    )


def crop_shape(array):
    count, width = array.shape
    return array.reshape(count // CROP, CROP, width // HS, HS)


def attend_forward(query, keys, values):
    scale = 1.0 / math.sqrt(HS)

    def one_crop(item):
        crop_query, crop_keys, crop_values = item
        scores = (
            jnp.einsum("qhd,khd->hqk", crop_query, crop_keys, preferred_element_type=jnp.float32)
            * scale
        )
        highest = jnp.max(scores, axis=-1, keepdims=True)
        weights = jnp.exp(scores - highest)
        total = jnp.sum(weights, axis=-1, keepdims=True)
        probs = (weights / total).astype(jnp.bfloat16)
        mixed = jnp.einsum("hqk,khd->qhd", probs, crop_values, preferred_element_type=jnp.float32)
        return (mixed.astype(jnp.bfloat16), (highest + jnp.log(total))[..., 0])

    mixed, logsum = lax.map(one_crop, (crop_shape(query), crop_shape(keys), crop_shape(values)))
    return (mixed.reshape(query.shape), logsum)


def attend_back(query, keys, values, logsum, upstream):
    scale = 1.0 / math.sqrt(HS)

    def one_crop(item):
        crop_query, crop_keys, crop_values, crop_logsum, crop_up = item
        scores = (
            jnp.einsum("qhd,khd->hqk", crop_query, crop_keys, preferred_element_type=jnp.float32)
            * scale
        )
        probs = jnp.exp(scores - crop_logsum[..., None])
        values_raw = jnp.einsum(
            "hqk,qhd->khd", probs.astype(jnp.bfloat16), crop_up, preferred_element_type=jnp.float32
        )
        probs_grad = jnp.einsum(
            "qhd,khd->hqk", crop_up, crop_values, preferred_element_type=jnp.float32
        )
        inner = jnp.sum(probs * probs_grad, axis=-1, keepdims=True)
        scores_grad = (probs * (probs_grad - inner)).astype(jnp.bfloat16)
        query_grad = (
            jnp.einsum("hqk,khd->qhd", scores_grad, crop_keys, preferred_element_type=jnp.float32)
            * scale
        )
        keys_grad = (
            jnp.einsum("hqk,qhd->khd", scores_grad, crop_query, preferred_element_type=jnp.float32)
            * scale
        )
        return (
            query_grad.astype(jnp.bfloat16),
            keys_grad.astype(jnp.bfloat16),
            values_raw.astype(jnp.bfloat16),
        )

    items = (crop_shape(query), crop_shape(keys), crop_shape(values), logsum, crop_shape(upstream))
    query_grad, keys_grad, values_grad = lax.map(one_crop, items)
    return (
        query_grad.reshape(query.shape),
        keys_grad.reshape(query.shape),
        values_grad.reshape(query.shape),
    )


def on_device(
    latents,
    cotangent,
    crop_counts,
    image_device,
    query_weight,
    key_weight,
    value_weight,
    out_weight,
    up_weight,
    down_weight,
    query_bias,
    value_bias,
    up_bias,
    out_bias,
    down_bias,
    first_gain,
    first_shift,
    second_gain,
    second_shift,
):
    count = latents.shape[0]
    owned = jnp.sum(jnp.where(image_device == lax.axis_index("wide"), crop_counts, 0))
    first_row = lax.axis_index("narrow") * count
    crop_index = (first_row + jnp.arange(count, dtype=jnp.int32)) // CROP
    live = (crop_index < owned).astype(jnp.float32)[:, None]
    query_full, key_full, value_full, up_full = (query_weight, key_weight, value_weight, up_weight)
    out_full, down_full = (out_weight, down_weight)
    qbias_full, vbias_full, upbias_full = (query_bias, value_bias, up_bias)
    latent_rows = latents.astype(jnp.float32)
    first_normed, first_unit, first_inverse = normalize(latent_rows, first_gain, first_shift)
    first_all = lax.all_gather(first_normed.astype(jnp.bfloat16), "narrow", axis=0, tiled=True)
    query = (matmul(first_all, query_full) + qbias_full).astype(jnp.bfloat16)
    keys = matmul(first_all, key_full).astype(jnp.bfloat16)
    values = (matmul(first_all, value_full) + vbias_full).astype(jnp.bfloat16)
    attended, logsum = attend_forward(query, keys, values)
    hidden = (
        latent_rows
        + lax.psum_scatter(
            matmul(attended, out_full).astype(jnp.bfloat16),
            "narrow",
            scatter_dimension=0,
            tiled=True,
        ).astype(jnp.float32)
        + out_bias
    )
    second_normed, second_unit, second_inverse = normalize(hidden, second_gain, second_shift)
    second_all = lax.all_gather(second_normed.astype(jnp.bfloat16), "narrow", axis=0, tiled=True)
    before = matmul(second_all, up_full) + upbias_full
    gelu_value, gelu_pull = jax.vjp(partial(jax.nn.gelu, approximate=False), before)
    activated = gelu_value.astype(jnp.bfloat16)
    result = (
        hidden
        + lax.psum_scatter(
            matmul(
                lax.dynamic_slice_in_dim(
                    activated, jnp.int32(0), lax.axis_size("narrow") * count, 0
                ),
                down_full,
            ).astype(jnp.bfloat16),
            "narrow",
            scatter_dimension=0,
            tiled=True,
        ).astype(jnp.float32)
        + down_bias
    )
    block_output = (result * live).astype(jnp.bfloat16)
    top_grad = cotangent.astype(jnp.float32) * live
    down_bias_grad = jnp.sum(top_grad, axis=0)
    top_all = lax.all_gather(top_grad.astype(jnp.bfloat16), "narrow", axis=0, tiled=True)
    down_grad = matmul_left(activated, top_all)
    activated_grad = matmul_right(top_all, down_full)
    before_grad = gelu_pull(activated_grad)[0].astype(jnp.bfloat16)
    upbias_grad = jnp.sum(before_grad.astype(jnp.float32), axis=0)
    up_grad = matmul_left(second_all, before_grad)
    second_grad = lax.psum_scatter(
        matmul_right(before_grad, up_full).astype(jnp.bfloat16),
        "narrow",
        scatter_dimension=0,
        tiled=True,
    ).astype(jnp.float32)
    hidden_part, second_gain_grad, second_shift_grad = normalize_back(
        second_grad, second_unit, second_inverse, second_gain
    )
    hidden_grad = top_grad + hidden_part
    out_bias_grad = jnp.sum(hidden_grad, axis=0)
    hidden_all = lax.all_gather(hidden_grad.astype(jnp.bfloat16), "narrow", axis=0, tiled=True)
    out_grad = matmul_left(attended, hidden_all)
    attended_grad = matmul_right(hidden_all, out_full).astype(jnp.bfloat16)
    query_grad, keys_grad, values_grad = attend_back(query, keys, values, logsum, attended_grad)
    qbias_grad = jnp.sum(query_grad.astype(jnp.float32), axis=0)
    vbias_grad = jnp.sum(values_grad.astype(jnp.float32), axis=0)
    query_wgrad = matmul_left(first_all, query_grad)
    key_wgrad = matmul_left(first_all, keys_grad)
    value_wgrad = matmul_left(first_all, values_grad)
    part = matmul_right(query_grad, query_full)
    part = part + matmul_right(keys_grad, key_full)
    first_grad = lax.psum_scatter(
        (part + matmul_right(values_grad, value_full)).astype(jnp.bfloat16),
        "narrow",
        scatter_dimension=0,
        tiled=True,
    ).astype(jnp.float32)
    input_part, first_gain_grad, first_shift_grad = normalize_back(
        first_grad, first_unit, first_inverse, first_gain
    )
    latents_gradient = hidden_grad + input_part
    matrices = (
        lax.psum(query_wgrad.astype(jnp.bfloat16), "wide").astype(jnp.float32),
        lax.psum(key_wgrad.astype(jnp.bfloat16), "wide").astype(jnp.float32),
        lax.psum(value_wgrad.astype(jnp.bfloat16), "wide").astype(jnp.float32),
        lax.psum(out_grad.astype(jnp.bfloat16), "wide").astype(jnp.float32),
        lax.psum(up_grad.astype(jnp.bfloat16), "wide").astype(jnp.float32),
        lax.psum(down_grad.astype(jnp.bfloat16), "wide").astype(jnp.float32),
        lax.psum(qbias_grad.astype(jnp.bfloat16), "wide").astype(jnp.float32),
        lax.psum(vbias_grad.astype(jnp.bfloat16), "wide").astype(jnp.float32),
        lax.psum(upbias_grad.astype(jnp.bfloat16), "wide").astype(jnp.float32),
    )
    rowwise = lax.psum(
        (
            first_gain_grad,
            first_shift_grad,
            second_gain_grad,
            second_shift_grad,
            out_bias_grad,
            down_bias_grad,
        ),
        ("wide", "narrow"),
    )
    return (
        block_output,
        latents_gradient,
        matrices[0],
        matrices[1],
        matrices[2],
        matrices[3],
        matrices[4],
        matrices[5],
        matrices[6],
        matrices[7],
        matrices[8],
        rowwise[4],
        rowwise[5],
        rowwise[0],
        rowwise[1],
        rowwise[2],
        rowwise[3],
    )


def solution(mesh):
    return jax.shard_map(
        on_device,
        mesh=mesh,
        in_specs=(
            P(("wide", "narrow"), None),
            P(("wide", "narrow"), None),
            P(),
            P(),
            P(None, "narrow"),
            P(None, "narrow"),
            P(None, "narrow"),
            P("narrow", None),
            P(None, "narrow"),
            P("narrow", None),
            P("narrow"),
            P("narrow"),
            P("narrow"),
            P(),
            P(),
            P(),
            P(),
            P(),
            P(),
        ),
        out_specs=(
            P(("wide", "narrow"), None),
            P(("wide", "narrow"), None),
            P(None, "narrow"),
            P(None, "narrow"),
            P(None, "narrow"),
            P("narrow", None),
            P(None, "narrow"),
            P("narrow", None),
            P("narrow"),
            P("narrow"),
            P("narrow"),
            P(),
            P(),
            P(),
            P(),
            P(),
            P(),
        ),
        check_vma=False,
    )
```

profile of v0, /device:TPU:0, one launch (start us, length us, event | category | flops | bytes accessed | tf_op | source)
XLA Modules:
  0.0 1423.9 jit_solution(12782932127262748092)
XLA Ops:
  17.3 106.6 %all-gather.5.cloned.1.call-done = bf16[4096,1024]{1,0:T(8,128)(2,1)} async-done(((bf16[2048,1024]{1,0:T(8,128)(2,1)}), bf16[4096,1024]{1,0:T(8,128)(2,1)}) %all-gather.5.cloned.1.call-update) | async-done | bytes 8388624 | tf_op jit(solution)/shard_map/all_gather | solution.py:140
  123.9 9.4 add_convert_fusion.3
  133.3 7.0 reshape.160
  140.3 5.3 copy.58
  145.6 9.4 add_convert_fusion.4
  155.0 7.0 reshape.159
  162.0 9.4 convolution_convert_fusion.4
  171.4 6.9 reshape.161
  178.3 5.2 copy.59
  185.9 53.5 %while.26 = (s32[]{:T(128)}, bf16[8,512,4,128]{1,3,2,0:T(8,128)(2,1)}, f32[8,4,512]{2,1,0:T(4,128)}, bf16[8,512,4,128]{3,2,1,0:T(4,128)(2,1)}, bf16[8,512,4,128]...) while((s32[]{:T(128)}, bf16[8,512,4,128]{1,3,2,0:T(8,128)(2,1)}, f32[8,4,512]{2,1,0:T(4,128)}, ...), condition=%wide.region_5.6_spmd, body=%wide.region_2.5_spmd.sunk | while | flops 546568192 | bytes 16843872 | solution.py:64
  239.5 4.7 copy.60
  248.3 6.8 convolution_convert_fusion.2
  255.2 99.4 %reduce-scatter.5.cloned.1.call-done = bf16[2048,1024]{1,0:T(8,128)(2,1)} async-done(((bf16[4096,1024]{1,0:T(8,128)(2,1)}), bf16[2048,1024]{1,0:T(8,128)(2,1)}) %reduce-scatter.5.cloned.1.call-update) | async-done | bytes 4194320 | tf_op jit(solution)/shard_map/reduce_scatter | solution.py:147
  354.7 5.0 fusion.79
  362.7 3.7 add_convert_fusion.2
  367.8 4.9 fusion.73
  373.3 97.3 %all-gather.7.cloned.1.call-done = bf16[4096,1024]{1,0:T(8,128)(2,1)} async-done(((bf16[2048,1024]{1,0:T(8,128)(2,1)}), bf16[4096,1024]{1,0:T(8,128)(2,1)}) %all-gather.7.cloned.1.call-update) | async-done | bytes 8388624 | tf_op jit(solution)/shard_map/all_gather | solution.py:156
  470.6 10.3 fusion.90
  480.9 95.1 %all-gather.9.cloned.1.call-done = bf16[4096,1024]{1,0:T(8,128)(2,1)} async-done(((bf16[2048,1024]{1,0:T(8,128)(2,1)}), bf16[4096,1024]{1,0:T(8,128)(2,1)}) %all-gather.9.cloned.1.call-update) | async-done | bytes 8388624 | tf_op jit(solution)/shard_map/all_gather | solution.py:178
  576.0 27.7 %fusion.88 = (bf16[512]{0:T(512)(128)(2,1)}, bf16[4096,512]{1,0:T(8,128)(2,1)S(1)}, f32[4096,512]{1,0:T(8,128)}) fusion(f32[4096,512]{1,0:T(8,128)} %fusion.90, f32[512]{0:T(512)S(1)} %convert_element_type.173, bf16[4096,1024]{1,0:T(8,128)(2,1)} %all-gather.9.cloned.1.call-done, bf16[512,1024]{1,0:T(8,128)(2,1)S(1)} %copy-done), kind=kOutput, calls=%fused_computation.149 | convolution fusion | flops 4450156032 | bytes 30411776 | tf_op jit(solution)/shard_map/dot_general | solution.py:38
  605.6 7.2 convolution_convert_fusion
  613.1 8.0 multiply_convert_fusion.2
  623.2 6.7 convolution_convert_fusion.1
  630.0 82.4 %reduce-scatter.9.cloned.1.call-done = bf16[2048,1024]{1,0:T(8,128)(2,1)} async-done(((bf16[4096,1024]{1,0:T(8,128)(2,1)}), bf16[2048,1024]{1,0:T(8,128)(2,1)}) %reduce-scatter.9.cloned.1.call-update) | async-done | bytes 4194320 | tf_op jit(solution)/shard_map/reduce_scatter | solution.py:184
  712.3 8.0 fusion.70
  720.4 94.1 %reduce-scatter.7.cloned.1.call-done = bf16[2048,1024]{1,0:T(8,128)(2,1)} async-done(((bf16[4096,1024]{1,0:T(8,128)(2,1)}), bf16[2048,1024]{1,0:T(8,128)(2,1)}) %reduce-scatter.7.cloned.1.call-update) | async-done | bytes 4194320 | tf_op jit(solution)/shard_map/reduce_scatter | solution.py:162
  814.4 12.4 fusion.86
  826.9 3.4 copy-done.5
  833.0 10.3 convolution_convert_fusion.5
  843.2 9.1 convolution_convert_fusion.6
  852.3 84.7 %all-gather.11.cloned.1.call-done = bf16[4096,1024]{1,0:T(8,128)(2,1)} async-done(((bf16[2048,1024]{1,0:T(8,128)(2,1)}), bf16[4096,1024]{1,0:T(8,128)(2,1)}) %all-gather.11.cloned.1.call-update) | async-done | bytes 8388624 | tf_op jit(solution)/shard_map/all_gather | solution.py:195
  937.0 9.5 convolution_convert_fusion.3
  946.6 6.9 reshape.163
  960.8 107.1 %while.27 = (s32[]{:T(128)}, bf16[8,512,4,128]{1,3,2,0:T(8,128)(2,1)}, bf16[8,512,4,128]{1,3,2,0:T(8,128)(2,1)}, bf16[8,512,4,128]{1,3,2,0:T(8,128)(2,1)}, bf16[...) while((s32[]{:T(128)}, ...), condition=%wide.region_16.17_spmd, body=%wide.region_14.16_spmd.sunk | while | flops 1356068864 | bytes 38857848 | solution.py:101
  1067.9 4.7 copy.66
  1084.4 9.6 fusion.92
  1094.0 8.4 convolution_convert_fusion.7
  1102.4 5.5 convolution_convert_fusion.9
  1107.9 5.5 convolution_convert_fusion.10
  1113.4 5.8 convolution_convert_fusion.8
  1119.3 10.8 fusion.91
  1130.1 18.8 %add_convert_fusion = bf16[4096,1024]{1,0:T(8,128)(2,1)} fusion(f32[4096,1024]{1,0:T(8,128)} %fusion.91, f32[4096,1024]{1,0:T(8,128)} %fusion.92, bf16[4096,512]{0,1:T(8,128)(2,1)} %bitcast.159, bf16[1024,512]{1,0:T(8,128)(2,1)S(1)} %copy-done.14), kind=kOutput, calls=%fused_computation.55 | convolution fusion | flops 4307550208 | bytes 47185920 | tf_op jit(solution)/shard_map/dot_general | solution.py:38
  1154.7 34.1 %all-reduce.1 = (bf16[512]{0:T(512)(128)(2,1)S(1)}, bf16[512]{0:T(512)(128)(2,1)S(1)}, bf16[512]{0:T(512)(128)(2,1)S(1)}) all-reduce(bf16[512]{0:T(512)(128)(2,1)S(1)} %bitcast.171, bf16[512]{0:T(512)(128)(2,1)S(1)} %bitcast.170, bf16[512]{0:T(512)(128)(2,1)S(1)} %copy-done.36), channel_id=1, replica_groups=mesh['wide'=16,'narrow'=2] {'wide'}, use_global_device_ids=true, to_apply=%region_27.28 | all-reduce | flops 1536 | bytes 6144 | tf_op jit(solution)/shard_map/psum | solution.py:223
  1190.5 68.9 %all-reduce.5.cloned.1.call-done = (bf16[1024,512]{1,0:T(8,128)(2,1)}, bf16[1024,512]{1,0:T(8,128)(2,1)}, bf16[1024,512]{1,0:T(8,128)(2,1)}, bf16[512,1024]{1,0:...) async-done(((bf16[1024,512]{1,0:T(8,128)(2,1)}, bf16[1024,512]{1,0:T(8,128)(2,1)}, bf16[1024,512]{1,0:T(8,128)(2,1)}, bf16[512,1024]{1,0:T(8,128)(2,1)}, ...) | async-done | bytes 6291472 | tf_op jit(solution)/shard_map/psum | solution.py:217
  1272.9 88.3 %reduce-scatter.11.cloned.1.call-done = bf16[2048,1024]{1,0:T(8,128)(2,1)} async-done(((bf16[4096,1024]{1,0:T(8,128)(2,1)}), bf16[2048,1024]{1,0:T(8,128)(2,1)}) %reduce-scatter.11.cloned.1.call-update) | async-done | bytes 4194320 | tf_op jit(solution)/shard_map/reduce_scatter | solution.py:206
  1361.2 6.1 fusion.71
  1367.4 40.0 %all-reduce = (f32[1024]{0:T(1024)}, f32[1024]{0:T(1024)}, f32[1024]{0:T(1024)}, f32[1024]{0:T(1024)}, f32[1024]{0:T(1024)}, /*index=5*/f32[1024]{0:T(1024)}) all-reduce(f32[1024]{0:T(1024)S(1)} %copy-done.28, f32[1024]{0:T(1024)S(1)} %copy-done.29, ...), channel_id=1, replica_groups=mesh['wide'=16,'narrow'=2] {'wide','narrow'}, use_global_device_ids=true, to_apply=%region_33.34 | all-reduce | flops 6144 | bytes 49152 | tf_op jit(solution)/shard_map/psum | solution.py:227
  1407.3 9.5 fusion.61
  (269 shorter events, 228.4 us)
Async XLA Ops:
  7.2 568.8 %copy-start = (bf16[512,1024]{1,0:T(8,128)(2,1)S(1)}, bf16[512,1024]{1,0:T(8,128)(2,1)}, u32[]{:S(2)}) copy-start(bf16[512,1024]{1,0:T(8,128)(2,1)} %param.32) | copy-start | bytes 3145732
  7.2 6.8 copy-start.23
  7.2 6.8 copy-start.30
  7.2 116.7 %all-gather.5.cloned.1.call-start = ((), (), s32[]{:S(2)}) async-start(), calls=%async_computation.4 | async-start | bytes 12582912 | tf_op jit(solution)/shard_map/all_gather | solution.py:140
  7.3 6.7 copy-start.2
  10.3 7.0 copy-start.33
  10.3 7.0 copy-start.34
  10.3 113.6 %copy-start.44 = (bf16[1024,512]{1,0:T(8,128)(2,1)S(1)}, bf16[1024,512]{1,0:T(8,128)(2,1)}, u32[]{:S(2)}) copy-start(bf16[1024,512]{1,0:T(8,128)(2,1)} %param.27) | copy-start | bytes 3145732
  17.0 337.6 %reduce-scatter.5.cloned.1.call-start = ((), (), s32[]{:S(2)}) async-start(), calls=%async_computation.5 | async-start | bytes 12582912 | tf_op jit(solution)/shard_map/reduce_scatter | solution.py:147
  133.3 12.3 copy-start.13
  155.0 7.0 copy-start.42
  239.5 8.9 copy-start.40
  255.1 99.5 %copy-start.22 = (f32[1024]{0:T(1024)S(1)}, f32[1024]{0:T(1024)}, u32[]{:S(2)}) copy-start(f32[1024]{0:T(1024)} %param.36) | copy-start | bytes 12292
  255.2 107.5 %copy-start.25 = (f32[1024]{0:T(1024)S(1)}, f32[1024]{0:T(1024)}, u32[]{:S(2)}) copy-start(f32[1024]{0:T(1024)} %param.40) | copy-start | bytes 12292
  255.2 107.5 %copy-start.31 = (f32[1024]{0:T(1024)S(1)}, f32[1024]{0:T(1024)}, u32[]{:S(2)}) copy-start(f32[1024]{0:T(1024)} %param.41) | copy-start | bytes 12292
  255.2 215.4 %all-gather.7.cloned.1.call-start = ((), (), s32[]{:S(2)}) async-start(), calls=%async_computation.6 | async-start | bytes 12582912 | tf_op jit(solution)/shard_map/all_gather | solution.py:156
  354.6 5.9 copy-start.4
  366.4 6.8 copy-start.35
  366.4 104.2 %copy-start.39 = (bf16[1024,512]{1,0:T(8,128)(2,1)S(1)}, bf16[1024,512]{1,0:T(8,128)(2,1)}, u32[]{:S(2)}) copy-start(bf16[1024,512]{1,0:T(8,128)(2,1)} %param.31) | copy-start | bytes 3145732
  366.5 209.5 %all-gather.9.cloned.1.call-start = ((), (), s32[]{:S(2)}) async-start(), calls=%async_computation.8 | async-start | bytes 12582912 | tf_op jit(solution)/shard_map/all_gather | solution.py:178
  372.7 339.6 %reduce-scatter.9.cloned.1.call-start = ((), (), s32[]{:S(2)}) async-start(), calls=%async_computation.9 | async-start | bytes 12582912 | tf_op jit(solution)/shard_map/reduce_scatter | solution.py:184
  612.8 201.6 %reduce-scatter.7.cloned.1.call-start = ((), (), s32[]{:S(2)}) async-start(), calls=%async_computation.7 | async-start | bytes 12582912 | tf_op jit(solution)/shard_map/reduce_scatter | solution.py:162
  629.9 184.5 %copy-start.32 = (f32[1024]{0:T(1024)S(1)}, f32[1024]{0:T(1024)}, u32[]{:S(2)}) copy-start(f32[1024]{0:T(1024)} %param.37) | copy-start | bytes 12292
  629.9 307.1 %all-gather.11.cloned.1.call-start = ((), (), s32[]{:S(2)}) async-start(), calls=%async_computation.10 | async-start | bytes 12582912 | tf_op jit(solution)/shard_map/all_gather | solution.py:195
  832.9 426.5 %all-reduce.5.cloned.1.call-start = ((), (), s32[]{:S(2)}) async-start(), calls=%async_computation.12 | async-start | bytes 12582912 | tf_op jit(solution)/shard_map/psum | solution.py:217
  832.9 10.3 copy-start.47
  843.2 93.8 %copy-start.41 = (bf16[512,1024]{1,0:T(8,128)(2,1)S(1)}, bf16[512,1024]{1,0:T(8,128)(2,1)}, u32[]{:S(2)}) copy-start(bf16[512,1024]{1,0:T(8,128)(2,1)} %param.30) | copy-start | bytes 3145732
  1067.9 7.0 copy-start.6
  1079.5 33.9 %copy-start.8 = (bf16[64,8,8,512]{3,1,2,0:T(8,128)(2,1)}, bf16[64,8,8,512]{3,1,2,0:T(8,128)(2,1)S(1)}, u32[]{:S(2)}) copy-start(bf16[64,8,8,512]{3,1,2,0:T(8,128)(2,1)S(1)} %copy.81) | copy-start | bytes 12582916
  1084.4 23.5 %copy-start.11 = (bf16[64,8,8,512]{3,1,2,0:T(8,128)(2,1)}, bf16[64,8,8,512]{3,1,2,0:T(8,128)(2,1)S(1)}, u32[]{:S(2)}) copy-start(bf16[64,8,8,512]{3,1,2,0:T(8,128)(2,1)S(1)} %copy.79) | copy-start | bytes 12582916
  1084.4 9.6 copy-start.10
  1084.4 17.9 %slice-start = ((s8[8388608]{0:T(1024)(128)(4,1)}), s8[4194304]{0:T(1024)(128)(4,1)S(1)}, s32[]{:S(2)}) async-start(s8[8388608]{0:T(1024)(128)(4,1)} %bitcast.172), calls=%async_computation.13 | async-start | bytes 8388608
  1094.0 8.4 slice-start.1
  1113.4 5.9 copy-start.45
  1119.3 10.9 copy-start.14
  1119.3 241.9 %reduce-scatter.11.cloned.1.call-start = ((), (), s32[]{:S(2)}) async-start(), calls=%async_computation.11 | async-start | bytes 12582912 | tf_op jit(solution)/shard_map/reduce_scatter | solution.py:206
  1148.9 5.8 copy-start.36
  1259.4 8.7 copy-start.17
  1259.4 10.3 copy-start.16
  1259.4 11.9 copy-start.15
  1262.4 98.8 %copy-start.19 = (f32[2048]{0:T(1024)S(1)}, f32[2048]{0:T(1024)}, u32[]{:S(2)}) copy-start(f32[2048]{0:T(1024)} %copy-done.18) | copy-start | bytes 24580
  1262.4 98.8 %copy-start.21 = (f32[2048]{0:T(1024)S(1)}, f32[2048]{0:T(1024)}, u32[]{:S(2)}) copy-start(f32[2048]{0:T(1024)} %copy-done.20) | copy-start | bytes 24580
  1262.4 98.8 %copy-start.24 = (f32[1024]{0:T(1024)S(1)}, f32[1024]{0:T(1024)}, u32[]{:S(2)}) copy-start(f32[1024]{0:T(1024)} %param.38) | copy-start | bytes 12292
  1268.1 99.2 %copy-start.26 = (f32[1024]{0:T(1024)S(1)}, f32[1024]{0:T(1024)}, u32[]{:S(2)}) copy-start(f32[1024]{0:T(1024)} %get-tuple-element.134) | copy-start | bytes 12292
  1268.1 99.2 %copy-start.27 = (f32[1024]{0:T(1024)S(1)}, f32[1024]{0:T(1024)}, u32[]{:S(2)}) copy-start(f32[1024]{0:T(1024)} %get-tuple-element.140) | copy-start | bytes 12292
  1268.1 99.2 %copy-start.28 = (f32[1024]{0:T(1024)S(1)}, f32[1024]{0:T(1024)}, u32[]{:S(2)}) copy-start(f32[1024]{0:T(1024)} %get-tuple-element.187) | copy-start | bytes 12292
  1268.1 99.2 %copy-start.29 = (f32[1024]{0:T(1024)S(1)}, f32[1024]{0:T(1024)}, u32[]{:S(2)}) copy-start(f32[1024]{0:T(1024)} %get-tuple-element.199) | copy-start | bytes 12292
  1367.3 49.5 %copy-start.1 = (bf16[512,1024]{1,0:T(8,128)(2,1)S(1)}, bf16[512,1024]{1,0:T(8,128)(2,1)}, u32[]{:S(2)}) copy-start(bf16[512,1024]{1,0:T(8,128)(2,1)} %param.32) | copy-start | bytes 3145732
  (11 other events, 35.3 us)
Sparse Core Ops, SparseCore 0:
  17.1 106.6 all-gather.4
  255.3 99.3 reduce-scatter.4
  366.6 103.9 all-gather.6
  472.0 103.9 all-gather.8
  613.0 99.3 reduce-scatter.8
  715.1 99.3 reduce-scatter.6
  833.0 103.9 all-gather.10
  1119.4 139.9 all-reduce.4
  1261.7 99.4 reduce-scatter.10
where the time goes:
time: 1430 us; the launch traced here: 1420 us
  waiting for transfers between devices  817 us (57%)
  matrix products  289 us (20%)
  other arithmetic  114 us (8%)
  local copies, waits for them, and re-layouts  113 us (8%)
  blocking collectives  74.1 us (5%)
  between operations  15 us (1%)
    all_gather x1, waiting for transfers between devices, on_device(): lax.all_gather(first_normed.astype(jnp.bfloat16), 'narrow', axis=0, tiled...  107 us
    reduce_scatter x1, waiting for transfers between devices, on_device(): lax.psum_scatter(matmul(attended, out_full).astype(jnp.bfloat16), 'narrow...  99.4 us
    all_gather x1, waiting for transfers between devices, on_device(): lax.all_gather(second_normed.astype(jnp.bfloat16), 'narrow', axis=0, tile...  97.3 us
    all_gather x1, waiting for transfers between devices, on_device(): lax.all_gather(top_grad.astype(jnp.bfloat16), 'narrow', axis=0, tiled=True)  95.1 us
    reduce_scatter x1, waiting for transfers between devices, on_device(): lax.psum_scatter(matmul(lax.dynamic_slice_in_dim(activated, jnp.int32(0),...  94.1 us
    reduce_scatter x1, waiting for transfers between devices, on_device(): lax.psum_scatter((part + matmul_right(values_grad, value_full)).astype(jn...  88.3 us
    all_gather x1, waiting for transfers between devices, on_device(): lax.all_gather(hidden_grad.astype(jnp.bfloat16), 'narrow', axis=0, tiled=...  84.7 us
    dot_general x6, matrix products, matmul_right(): lax.dot_general(left, right, (((1,), (1,)), ((), ())), preferred_element_...  83.6 us
  transfers between devices with their start and end apart: 9, of which 9 were waited for; matrix products, arithmetic and copies ran while one was open for 8% of the time, Pallas kernels for 0%

commit v1 on v0

--- a/solution.py
+++ b/solution.py
@@ -220,7 +220,9 @@
         lax.psum(out_grad.astype(jnp.bfloat16), "wide").astype(jnp.float32),
         lax.psum(up_grad.astype(jnp.bfloat16), "wide").astype(jnp.float32),
         lax.psum(down_grad.astype(jnp.bfloat16), "wide").astype(jnp.float32),
-        lax.psum(qbias_grad.astype(jnp.bfloat16), "wide").astype(jnp.float32),
+        jnp.sum(lax.all_gather(qbias_grad.astype(jnp.bfloat16), "wide"), axis=0).astype(
+            jnp.float32
+        ),
         lax.psum(vbias_grad.astype(jnp.bfloat16), "wide").astype(jnp.float32),
         lax.psum(upbias_grad.astype(jnp.bfloat16), "wide").astype(jnp.float32),
     )

time: 1430 us -> 1430 us (level)
  blocking collectives: 74.1 us -> 91.3 us
  waiting for transfers between devices: 817 us -> 800 us
    all_gather x0 -> x1, blocking collectives: none -> 17.4 us  [on_device(): lax.all_gather(qbias_grad.astype(jnp.bfloat16), 'wide')]
    psum x1, waiting for transfers between devices: 68.9 us -> 51.5 us  [on_device(): lax.psum(query_wgrad.astype(jnp.bfloat16), 'wide').astype(jnp.float32)]
where the time goes in v1:
time: 1430 us; the launch traced here: 1420 us
  waiting for transfers between devices  800 us (56%)
  matrix products  289 us (20%)
  other arithmetic  114 us (8%)
  local copies, waits for them, and re-layouts  113 us (8%)
  blocking collectives  91.3 us (6%)
  between operations  15 us (1%)
    all_gather x1, waiting for transfers between devices, on_device(): lax.all_gather(first_normed.astype(jnp.bfloat16), 'narrow', axis=0, tiled...  107 us
    reduce_scatter x1, waiting for transfers between devices, on_device(): lax.psum_scatter(matmul(attended, out_full).astype(jnp.bfloat16), 'narrow...  99.4 us
    all_gather x1, waiting for transfers between devices, on_device(): lax.all_gather(second_normed.astype(jnp.bfloat16), 'narrow', axis=0, tile...  97.3 us
    all_gather x1, waiting for transfers between devices, on_device(): lax.all_gather(top_grad.astype(jnp.bfloat16), 'narrow', axis=0, tiled=True)  95.2 us
    reduce_scatter x1, waiting for transfers between devices, on_device(): lax.psum_scatter(matmul(lax.dynamic_slice_in_dim(activated, jnp.int32(0),...  94.1 us
    reduce_scatter x1, waiting for transfers between devices, on_device(): lax.psum_scatter((part + matmul_right(values_grad, value_full)).astype(jn...  88.3 us
    all_gather x1, waiting for transfers between devices, on_device(): lax.all_gather(hidden_grad.astype(jnp.bfloat16), 'narrow', axis=0, tiled=...  84.7 us
    dot_general x6, matrix products, matmul_right(): lax.dot_general(left, right, (((1,), (1,)), ((), ())), preferred_element_...  83.5 us
  transfers between devices with their start and end apart: 9, of which 9 were waited for; matrix products, arithmetic and copies ran while one was open for 8% of the time, Pallas kernels for 0%

profile of v1, /device:TPU:0, one launch (start us, length us, event | category | flops | bytes accessed | tf_op | source)
XLA Modules:
  0.0 1424.1 jit_solution(4943126281354545208)
XLA Ops:
  17.3 106.6 %all-gather.6.cloned.1.call-done = bf16[4096,1024]{1,0:T(8,128)(2,1)} async-done(((bf16[2048,1024]{1,0:T(8,128)(2,1)}), bf16[4096,1024]{1,0:T(8,128)(2,1)}) %all-gather.6.cloned.1.call-update) | async-done | bytes 8388624 | tf_op jit(solution)/shard_map/all_gather | solution.py:140
  123.9 9.4 add_convert_fusion.3
  133.3 7.0 reshape.161
  140.3 5.3 copy.76
  145.5 9.4 add_convert_fusion.4
  155.0 7.0 reshape.160
  161.9 9.4 convolution_convert_fusion.4
  171.3 6.9 reshape.162
  178.2 5.2 copy.77
  185.9 53.5 %while.26 = (s32[]{:T(128)}, bf16[8,512,4,128]{1,3,2,0:T(8,128)(2,1)}, f32[8,4,512]{2,1,0:T(4,128)}, bf16[8,512,4,128]{3,2,1,0:T(4,128)(2,1)}, bf16[8,512,4,128]...) while((s32[]{:T(128)}, bf16[8,512,4,128]{1,3,2,0:T(8,128)(2,1)}, f32[8,4,512]{2,1,0:T(4,128)}, ...), condition=%wide.region_5.6_spmd, body=%wide.region_2.5_spmd.sunk | while | flops 546568192 | bytes 16843872 | solution.py:64
  239.5 4.7 copy.78
  248.3 6.8 convolution_convert_fusion.2
  255.2 99.4 %reduce-scatter.5.cloned.1.call-done = bf16[2048,1024]{1,0:T(8,128)(2,1)} async-done(((bf16[4096,1024]{1,0:T(8,128)(2,1)}), bf16[2048,1024]{1,0:T(8,128)(2,1)}) %reduce-scatter.5.cloned.1.call-update) | async-done | bytes 4194320 | tf_op jit(solution)/shard_map/reduce_scatter | solution.py:147
  354.6 5.0 fusion.79
  362.7 3.7 add_convert_fusion.2
  367.8 4.9 fusion.73
  373.2 97.3 %all-gather.8.cloned.1.call-done = bf16[4096,1024]{1,0:T(8,128)(2,1)} async-done(((bf16[2048,1024]{1,0:T(8,128)(2,1)}), bf16[4096,1024]{1,0:T(8,128)(2,1)}) %all-gather.8.cloned.1.call-update) | async-done | bytes 8388624 | tf_op jit(solution)/shard_map/all_gather | solution.py:156
  470.6 10.3 fusion.90
  480.8 95.2 %all-gather.10.cloned.1.call-done = bf16[4096,1024]{1,0:T(8,128)(2,1)} async-done(((bf16[2048,1024]{1,0:T(8,128)(2,1)}), bf16[4096,1024]{1,0:T(8,128)(2,1)}) %all-gather.10.cloned.1.call-update) | async-done | bytes 8388624 | tf_op jit(solution)/shard_map/all_gather | solution.py:178
  576.0 27.7 %fusion.88 = (bf16[512]{0:T(512)(128)(2,1)}, bf16[4096,512]{1,0:T(8,128)(2,1)S(1)}, f32[4096,512]{1,0:T(8,128)}) fusion(f32[4096,512]{1,0:T(8,128)} %fusion.90, f32[512]{0:T(512)S(1)} %convert_element_type.175, bf16[4096,1024]{1,0:T(8,128)(2,1)} %all-gather.10.cloned.1.call-done, bf16[512,1024]{1,0:T(8,128)(2,1)S(1)} %copy-done), kind=kOutput, calls=%fused_computation.149 | convolution fusion | flops 4450156032 | bytes 30411776 | tf_op jit(solution)/shard_map/dot_general | solution.py:38
  605.6 7.2 convolution_convert_fusion
  613.0 8.0 multiply_convert_fusion.2
  623.1 6.7 convolution_convert_fusion.1
  629.9 82.4 %reduce-scatter.9.cloned.1.call-done = bf16[2048,1024]{1,0:T(8,128)(2,1)} async-done(((bf16[4096,1024]{1,0:T(8,128)(2,1)}), bf16[2048,1024]{1,0:T(8,128)(2,1)}) %reduce-scatter.9.cloned.1.call-update) | async-done | bytes 4194320 | tf_op jit(solution)/shard_map/reduce_scatter | solution.py:184
  712.3 8.0 fusion.70
  720.3 94.1 %reduce-scatter.7.cloned.1.call-done = bf16[2048,1024]{1,0:T(8,128)(2,1)} async-done(((bf16[4096,1024]{1,0:T(8,128)(2,1)}), bf16[2048,1024]{1,0:T(8,128)(2,1)}) %reduce-scatter.7.cloned.1.call-update) | async-done | bytes 4194320 | tf_op jit(solution)/shard_map/reduce_scatter | solution.py:162
  814.4 12.4 fusion.86
  832.9 10.3 convolution_convert_fusion.5
  843.2 9.1 convolution_convert_fusion.6
  852.3 84.7 %all-gather.12.cloned.1.call-done = bf16[4096,1024]{1,0:T(8,128)(2,1)} async-done(((bf16[2048,1024]{1,0:T(8,128)(2,1)}), bf16[4096,1024]{1,0:T(8,128)(2,1)}) %all-gather.12.cloned.1.call-update) | async-done | bytes 8388624 | tf_op jit(solution)/shard_map/all_gather | solution.py:195
  937.0 9.5 convolution_convert_fusion.3
  946.6 6.9 reshape.164
  960.8 107.2 %while.27 = (s32[]{:T(128)}, bf16[8,512,4,128]{1,3,2,0:T(8,128)(2,1)}, bf16[8,512,4,128]{1,3,2,0:T(8,128)(2,1)}, bf16[8,512,4,128]{1,3,2,0:T(8,128)(2,1)}, bf16[...) while((s32[]{:T(128)}, ...), condition=%wide.region_16.17_spmd, body=%wide.region_14.16_spmd.sunk | while | flops 1356068864 | bytes 38857848 | solution.py:101
  1067.9 4.7 copy.84
  1084.5 9.6 fusion.92
  1094.0 8.4 convolution_convert_fusion.7
  1102.4 5.5 convolution_convert_fusion.9
  1107.9 5.5 convolution_convert_fusion.10
  1113.5 5.8 convolution_convert_fusion.8
  1119.3 10.8 fusion.91
  1130.2 18.8 %add_convert_fusion = bf16[4096,1024]{1,0:T(8,128)(2,1)} fusion(f32[4096,1024]{1,0:T(8,128)} %fusion.91, f32[4096,1024]{1,0:T(8,128)} %fusion.92, bf16[4096,512]{0,1:T(8,128)(2,1)} %bitcast.158, bf16[1024,512]{1,0:T(8,128)(2,1)S(1)} %copy-done.14), kind=kOutput, calls=%fused_computation.55 | convolution fusion | flops 4307550208 | bytes 47185920 | tf_op jit(solution)/shard_map/dot_general | solution.py:38
  1154.8 33.9 %all-reduce.1 = (bf16[512]{0:T(512)(128)(2,1)S(1)}, bf16[512]{0:T(512)(128)(2,1)S(1)}) all-reduce(bf16[512]{0:T(512)(128)(2,1)S(1)} %bitcast.169, bf16[512]{0:T(512)(128)(2,1)S(1)} %copy-done.36), channel_id=1, replica_groups=mesh['wide'=16,'narrow'=2] {'wide'}, use_global_device_ids=true, to_apply=%region_29.30 | all-reduce | flops 1024 | bytes 4096 | tf_op jit(solution)/shard_map/psum | solution.py:226
  1189.8 17.4 %all-gather = bf16[16,1,512]{2,1,0:T(2,128)(2,1)S(1)} all-gather(bf16[1,1,512]{2,1,0:T(2,128)(2,1)S(1)} %reshape.168), channel_id=1, replica_groups=mesh['wide'=16,'narrow'=2] {'wide'}, dimensions={0}, use_global_device_ids=true | all-gather | bytes 17408 | tf_op jit(solution)/shard_map/all_gather | solution.py:223
  1207.9 51.5 %all-reduce.5.cloned.1.call-done = (bf16[1024,512]{1,0:T(8,128)(2,1)}, bf16[1024,512]{1,0:T(8,128)(2,1)}, bf16[1024,512]{1,0:T(8,128)(2,1)}, bf16[512,1024]{1,0:...) async-done(((bf16[1024,512]{1,0:T(8,128)(2,1)}, bf16[1024,512]{1,0:T(8,128)(2,1)}, bf16[1024,512]{1,0:T(8,128)(2,1)}, bf16[512,1024]{1,0:T(8,128)(2,1)}, ...) | async-done | bytes 6291472 | tf_op jit(solution)/shard_map/psum | solution.py:217
  1272.8 88.3 %reduce-scatter.11.cloned.1.call-done = bf16[2048,1024]{1,0:T(8,128)(2,1)} async-done(((bf16[4096,1024]{1,0:T(8,128)(2,1)}), bf16[2048,1024]{1,0:T(8,128)(2,1)}) %reduce-scatter.11.cloned.1.call-update) | async-done | bytes 4194320 | tf_op jit(solution)/shard_map/reduce_scatter | solution.py:206
  1361.2 6.4 fusion.71
  1367.6 40.0 %all-reduce = (f32[1024]{0:T(1024)}, f32[1024]{0:T(1024)}, f32[1024]{0:T(1024)}, f32[1024]{0:T(1024)}, f32[1024]{0:T(1024)}, /*index=5*/f32[1024]{0:T(1024)}) all-reduce(f32[1024]{0:T(1024)S(1)} %copy-done.28, f32[1024]{0:T(1024)S(1)} %copy-done.29, ...), channel_id=1, replica_groups=mesh['wide'=16,'narrow'=2] {'wide','narrow'}, use_global_device_ids=true, to_apply=%region_33.34 | all-reduce | flops 6144 | bytes 49152 | tf_op jit(solution)/shard_map/psum | solution.py:229
  1407.5 9.5 fusion.61
  (272 shorter events, 231.9 us)
Async XLA Ops:
  7.2 568.8 %copy-start = (bf16[512,1024]{1,0:T(8,128)(2,1)S(1)}, bf16[512,1024]{1,0:T(8,128)(2,1)}, u32[]{:S(2)}) copy-start(bf16[512,1024]{1,0:T(8,128)(2,1)} %param.32) | copy-start | bytes 3145732
  7.2 6.8 copy-start.23
  7.2 6.8 copy-start.30
  7.2 116.7 %all-gather.6.cloned.1.call-start = ((), (), s32[]{:S(2)}) async-start(), calls=%async_computation.4 | async-start | bytes 12582912 | tf_op jit(solution)/shard_map/all_gather | solution.py:140
  7.3 6.7 copy-start.2
  10.3 7.0 copy-start.33
  10.3 7.0 copy-start.34
  10.3 113.6 %copy-start.44 = (bf16[1024,512]{1,0:T(8,128)(2,1)S(1)}, bf16[1024,512]{1,0:T(8,128)(2,1)}, u32[]{:S(2)}) copy-start(bf16[1024,512]{1,0:T(8,128)(2,1)} %param.27) | copy-start | bytes 3145732
  17.0 337.6 %reduce-scatter.5.cloned.1.call-start = ((), (), s32[]{:S(2)}) async-start(), calls=%async_computation.5 | async-start | bytes 12582912 | tf_op jit(solution)/shard_map/reduce_scatter | solution.py:147
  133.3 12.2 copy-start.13
  155.0 7.0 copy-start.42
  239.5 8.8 copy-start.40
  255.1 99.5 %copy-start.22 = (f32[1024]{0:T(1024)S(1)}, f32[1024]{0:T(1024)}, u32[]{:S(2)}) copy-start(f32[1024]{0:T(1024)} %param.36) | copy-start | bytes 12292
  255.1 107.5 %copy-start.25 = (f32[1024]{0:T(1024)S(1)}, f32[1024]{0:T(1024)}, u32[]{:S(2)}) copy-start(f32[1024]{0:T(1024)} %param.40) | copy-start | bytes 12292
  255.2 107.5 %copy-start.31 = (f32[1024]{0:T(1024)S(1)}, f32[1024]{0:T(1024)}, u32[]{:S(2)}) copy-start(f32[1024]{0:T(1024)} %param.41) | copy-start | bytes 12292
  255.2 215.4 %all-gather.8.cloned.1.call-start = ((), (), s32[]{:S(2)}) async-start(), calls=%async_computation.6 | async-start | bytes 12582912 | tf_op jit(solution)/shard_map/all_gather | solution.py:156
  354.6 5.9 copy-start.4
  366.4 6.8 copy-start.35
  366.4 104.2 %copy-start.39 = (bf16[1024,512]{1,0:T(8,128)(2,1)S(1)}, bf16[1024,512]{1,0:T(8,128)(2,1)}, u32[]{:S(2)}) copy-start(bf16[1024,512]{1,0:T(8,128)(2,1)} %param.31) | copy-start | bytes 3145732
  366.4 209.6 %all-gather.10.cloned.1.call-start = ((), (), s32[]{:S(2)}) async-start(), calls=%async_computation.8 | async-start | bytes 12582912 | tf_op jit(solution)/shard_map/all_gather | solution.py:178
  372.7 339.6 %reduce-scatter.9.cloned.1.call-start = ((), (), s32[]{:S(2)}) async-start(), calls=%async_computation.9 | async-start | bytes 12582912 | tf_op jit(solution)/shard_map/reduce_scatter | solution.py:184
  612.8 201.6 %reduce-scatter.7.cloned.1.call-start = ((), (), s32[]{:S(2)}) async-start(), calls=%async_computation.7 | async-start | bytes 12582912 | tf_op jit(solution)/shard_map/reduce_scatter | solution.py:162
  629.9 184.5 %copy-start.32 = (f32[1024]{0:T(1024)S(1)}, f32[1024]{0:T(1024)}, u32[]{:S(2)}) copy-start(f32[1024]{0:T(1024)} %param.37) | copy-start | bytes 12292
  629.9 307.1 %all-gather.12.cloned.1.call-start = ((), (), s32[]{:S(2)}) async-start(), calls=%async_computation.10 | async-start | bytes 12582912 | tf_op jit(solution)/shard_map/all_gather | solution.py:195
  832.9 426.5 %all-reduce.5.cloned.1.call-start = ((), (), s32[]{:S(2)}) async-start(), calls=%async_computation.12 | async-start | bytes 12582912 | tf_op jit(solution)/shard_map/psum | solution.py:217
  832.9 10.3 copy-start.47
  843.2 93.8 %copy-start.41 = (bf16[512,1024]{1,0:T(8,128)(2,1)S(1)}, bf16[512,1024]{1,0:T(8,128)(2,1)}, u32[]{:S(2)}) copy-start(bf16[512,1024]{1,0:T(8,128)(2,1)} %param.30) | copy-start | bytes 3145732
  1067.9 7.0 copy-start.6
  1079.6 33.9 %copy-start.8 = (bf16[64,8,8,512]{3,1,2,0:T(8,128)(2,1)}, bf16[64,8,8,512]{3,1,2,0:T(8,128)(2,1)S(1)}, u32[]{:S(2)}) copy-start(bf16[64,8,8,512]{3,1,2,0:T(8,128)(2,1)S(1)} %copy.99) | copy-start | bytes 12582916
  1084.4 23.5 %copy-start.11 = (bf16[64,8,8,512]{3,1,2,0:T(8,128)(2,1)}, bf16[64,8,8,512]{3,1,2,0:T(8,128)(2,1)S(1)}, u32[]{:S(2)}) copy-start(bf16[64,8,8,512]{3,1,2,0:T(8,128)(2,1)S(1)} %copy.97) | copy-start | bytes 12582916
  1084.5 9.6 copy-start.10
  1084.5 17.9 %slice-start = ((s8[8388608]{0:T(1024)(128)(4,1)}), s8[4194304]{0:T(1024)(128)(4,1)S(1)}, s32[]{:S(2)}) async-start(s8[8388608]{0:T(1024)(128)(4,1)} %bitcast.170), calls=%async_computation.13 | async-start | bytes 8388608
  1094.0 8.4 slice-start.1
  1113.5 5.9 copy-start.45
  1119.3 10.9 copy-start.14
  1119.3 241.9 %reduce-scatter.11.cloned.1.call-start = ((), (), s32[]{:S(2)}) async-start(), calls=%async_computation.11 | async-start | bytes 12582912 | tf_op jit(solution)/shard_map/reduce_scatter | solution.py:206
  1149.0 5.8 copy-start.36
  1259.3 8.7 copy-start.17
  1259.3 10.3 copy-start.16
  1259.3 11.9 copy-start.15
  1262.3 98.8 %copy-start.19 = (f32[2048]{0:T(1024)S(1)}, f32[2048]{0:T(1024)}, u32[]{:S(2)}) copy-start(f32[2048]{0:T(1024)} %copy-done.18) | copy-start | bytes 24580
  1262.3 98.8 %copy-start.21 = (f32[2048]{0:T(1024)S(1)}, f32[2048]{0:T(1024)}, u32[]{:S(2)}) copy-start(f32[2048]{0:T(1024)} %copy-done.20) | copy-start | bytes 24580
  1262.3 98.8 %copy-start.24 = (f32[1024]{0:T(1024)S(1)}, f32[1024]{0:T(1024)}, u32[]{:S(2)}) copy-start(f32[1024]{0:T(1024)} %param.38) | copy-start | bytes 12292
  1268.1 99.5 %copy-start.26 = (f32[1024]{0:T(1024)S(1)}, f32[1024]{0:T(1024)}, u32[]{:S(2)}) copy-start(f32[1024]{0:T(1024)} %get-tuple-element.149) | copy-start | bytes 12292
  1268.1 99.5 %copy-start.27 = (f32[1024]{0:T(1024)S(1)}, f32[1024]{0:T(1024)}, u32[]{:S(2)}) copy-start(f32[1024]{0:T(1024)} %get-tuple-element.155) | copy-start | bytes 12292
  1268.1 99.5 %copy-start.28 = (f32[1024]{0:T(1024)S(1)}, f32[1024]{0:T(1024)}, u32[]{:S(2)}) copy-start(f32[1024]{0:T(1024)} %get-tuple-element.201) | copy-start | bytes 12292
  1268.1 99.5 %copy-start.29 = (f32[1024]{0:T(1024)S(1)}, f32[1024]{0:T(1024)}, u32[]{:S(2)}) copy-start(f32[1024]{0:T(1024)} %get-tuple-element.213) | copy-start | bytes 12292
  1367.6 49.5 %copy-start.1 = (bf16[512,1024]{1,0:T(8,128)(2,1)S(1)}, bf16[512,1024]{1,0:T(8,128)(2,1)}, u32[]{:S(2)}) copy-start(bf16[512,1024]{1,0:T(8,128)(2,1)} %param.32) | copy-start | bytes 3145732
  (11 other events, 35.3 us)
Sparse Core Ops, SparseCore 0:
  17.1 106.6 all-gather.5
  255.3 99.3 reduce-scatter.4
  366.6 103.9 all-gather.7
  472.0 103.9 all-gather.9
  612.9 99.3 reduce-scatter.8
  715.0 99.3 reduce-scatter.6
  833.0 103.9 all-gather.11
  1119.4 139.8 all-reduce.4
  1261.6 99.4 reduce-scatter.10
